TPU v7x, 256 devices: a whole 4x4x8 slice. The times are simulated.
256 devices in a mesh: obs: 32 (over z, x_hi, core), ind: 8 (over y, x_lo).
Axes of the slice: x: 4 (x_hi: 2, x_lo: 2; x = x_hi * 2 + x_lo), y: 4, z: 8, core: 2. Of those that a mesh axis runs over, the one named last changes fastest.
Arguments:
- obs_coords: float32 [2, 131072], P(None, 'obs'), may hold values from 0 to 1
- obs_codes: int32 [131072], P('obs'), may hold values from 0 to 47
- route_plan: int32 [32, 32], replicated, may hold values from 0 to 1, as said below
- inducing_coords: float32 [2, 8192], P(None, 'ind'), may hold values from 0 to 1
- inducing_bands: int32 [8192], P('ind'), may hold values from 0 to 5
- band_mix: float32 [6, 6], replicated, may hold values from -2.4 to 2.4
- lengthscales: float32 [2], replicated, may hold values from 0.04 to 0.1
- class_scales: float32 [8], replicated, may hold values from 0.5 to 2
- prior_factor: bfloat16 [8192, 1024], P(('ind', 'obs')), may hold values from -0.046875 to 0.046875
- variational_chol: bfloat16 [8192, 1024], P(('ind', 'obs')), may hold values from -1 to 1, as said below
- variational_mean: bfloat16 [8, 8192], P(None, 'ind'), may hold values from -6 to 6
Outputs:
- class_probs: float32 [8, 65536], P(None, 'obs')
- grad_chol: float32 [8192, 1024], P(('ind', 'obs'))
- grad_mean: float32 [8, 8192], P(None, 'ind')
Inputs may be any that keep to these rules, and one draw needn't show every extreme that they name: `route_plan`: entry [s, d] is the number of 128-row blocks that reader s hands to device d; every column sums to 16; a reader's blocks go out in order of destination from the front of its buffer. `variational_chol`: each block's rows are lower triangular within the block, with diagonal entries of 0.3 to 1.
All inputs are finite; a program needn't handle non-finite values.
Results may differ from a plain program's by a relative error of at most 0.014.
Values may be sent and summed in bfloat16 or wider, within the bound.
A program may use at most 64 MiB of HBM per device.

v0:
```python
import jax
import jax.numpy as jnp
from jax import lax
from jax.sharding import PartitionSpec as P

C = 8
NB = 6
ROWS_DEV = 2048
precise = lax.Precision.HIGHEST


def cross_cov(coords, band_ids, centers, center_bands, lengthscales, coupling):
    delta_t = (coords[0][:, None] - centers[0][None, :]) / lengthscales[0]
    delta_w = (coords[1][:, None] - centers[1][None, :]) / lengthscales[1]
    kinds = jnp.arange(NB, dtype=jnp.int32)
    row_hot = (band_ids[:, None] == kinds[None, :]).astype(jnp.float32)
    col_hot = (center_bands[:, None] == kinds[None, :]).astype(jnp.float32)
    mixing = jnp.dot(jnp.dot(row_hot, coupling, precision=precise), col_hot.T, precision=precise)
    return (jnp.exp(-0.5 * (delta_t * delta_t + delta_w * delta_w)) * mixing).astype(jnp.bfloat16)


def likelihood(mean_sum, variance, class_scales):
    logits = mean_sum + 0.5 * class_scales[:, None] * variance[None, :]
    weights = jnp.exp(logits)
    chances = weights / jnp.sum(weights, axis=0, keepdims=True)
    var_slope = -0.5 * jnp.sum(chances * class_scales[:, None], axis=0)
    return (chances, var_slope)


def body(
    obs_coords,
    obs_codes,
    route_plan,
    inducing_coords,
    inducing_bands,
    band_mix,
    lengthscales,
    class_scales,
    prior_factor,
    variational_chol,
    variational_mean,
):
    devices = lax.axis_size("obs")
    my_index = lax.axis_index("obs")
    slot_rows = 128
    blocks = route_plan * slot_rows
    send_start = jnp.cumsum(blocks, axis=1) - blocks
    recv_start = jnp.cumsum(blocks, axis=0) - blocks
    my_sends = lax.dynamic_index_in_dim(send_start, my_index, 0, keepdims=False)
    my_recvs = lax.dynamic_index_in_dim(recv_start, my_index, 1, keepdims=False)
    stacked = jnp.concatenate([obs_coords, obs_codes.astype(jnp.float32)[None, :]], axis=0)
    padded = jnp.concatenate([stacked, jnp.zeros((3, slot_rows), jnp.float32)], axis=1)
    outgoing = jax.vmap(lambda offset: lax.dynamic_slice_in_dim(padded, offset, slot_rows, 1))(
        my_sends
    )
    incoming = lax.all_to_all(outgoing, "obs", split_axis=0, concat_axis=0, tiled=True)
    position = jnp.arange(ROWS_DEV, dtype=jnp.int32)
    sources = jnp.arange(devices, dtype=jnp.int32)
    source = jnp.sum((my_recvs[None, :] <= position[:, None]).astype(jnp.int32), axis=1) - 1
    pick = (source[:, None] == sources[None, :]).astype(jnp.int32)
    begin_row = jnp.sum(pick * my_recvs[None, :], axis=1)
    arrived = incoming[source, :, position - begin_row].T
    coords = arrived[0:2]
    code_ids = arrived[2].astype(jnp.int32)
    band_ids = code_ids % NB
    labels = code_ids // NB
    coupling = jnp.eye(NB, dtype=jnp.float32) + jnp.dot(band_mix, band_mix.T, precision=precise)
    kinds = jnp.arange(NB, dtype=jnp.int32)
    row_hot = (band_ids[:, None] == kinds[None, :]).astype(jnp.float32)
    self_cov = jnp.sum(row_hot * jnp.dot(row_hot, coupling, precision=precise), axis=1)
    kernel_rows = cross_cov(
        coords, band_ids, inducing_coords, inducing_bands, lengthscales, coupling
    )
    prior_block, chol_block = (
        lax.all_gather(prior_factor, "obs", axis=0, tiled=True),
        lax.all_gather(variational_chol, "obs", axis=0, tiled=True),
    )
    whitened = jnp.dot(kernel_rows, prior_block, preferred_element_type=jnp.float32)
    whitened_bf = whitened.astype(jnp.bfloat16)
    covariant = jnp.dot(whitened_bf, chol_block, preferred_element_type=jnp.float32)
    mean_part = lax.dot_general(
        variational_mean, whitened_bf, (((1,), (1,)), ((), ())), preferred_element_type=jnp.float32
    )
    var_part = (jnp.sum(covariant * covariant, axis=1) - jnp.sum(whitened * whitened, axis=1))[
        None, :
    ]
    mean_sum, var_sum = lax.psum((mean_part, var_part), "ind")
    chances, var_slope = likelihood(mean_sum, self_cov + var_sum[0], class_scales)
    classes = jnp.arange(C, dtype=jnp.int32)
    mean_slope = ((labels[None, :] == classes[:, None]).astype(jnp.float32) - chances).astype(
        jnp.bfloat16
    )
    heavy = (2.0 * var_slope[:, None] * covariant).astype(jnp.bfloat16)
    piece_rows = variational_chol.shape[0]
    full_width = variational_chol.shape[1]
    column_ids = jnp.arange(full_width, dtype=jnp.int32)
    own_rows = my_index * piece_rows + jnp.arange(piece_rows, dtype=jnp.int32)[:, None]
    term = lax.dot_general(
        whitened_bf, heavy, (((0,), (0,)), ((), ())), preferred_element_type=jnp.float32
    )
    row_ids = jnp.arange(lax.axis_size("obs") * piece_rows, dtype=jnp.int32)[:, None]
    data_term = lax.psum_scatter(
        jnp.where(column_ids[None, :] <= row_ids, term, 0.0).astype(jnp.bfloat16),
        "obs",
        scatter_dimension=0,
        tiled=True,
    ).astype(jnp.float32)
    on_diag = column_ids[None, :] == own_rows
    own_chol = variational_chol.astype(jnp.float32)
    diagonal = jnp.sum(jnp.where(on_diag, own_chol, 0.0), axis=1, keepdims=True)
    grad_chol = data_term - own_chol + jnp.where(on_diag, 1.0 / diagonal, 0.0)
    mean_term = lax.dot_general(
        mean_slope, whitened_bf, (((1,), (0,)), ((), ())), preferred_element_type=jnp.float32
    )
    grad_mean = lax.psum(mean_term, "obs") - variational_mean.astype(jnp.float32)
    return (chances, grad_chol, grad_mean)


def solution(mesh):
    placed = (
        P(None, "obs"),
        P("obs"),
        P(),
        P(None, "ind"),
        P("ind"),
        P(),
        P(),
        P(),
        P(("ind", "obs"), None),
        P(("ind", "obs"), None),
        P(None, "ind"),
    )
    return jax.shard_map(
        body,
        mesh=mesh,
        in_specs=placed,
        out_specs=(P(None, "obs"), P(("ind", "obs"), None), P(None, "ind")),
        check_vma=False,
    )
```

profile of v0, /device:TPU:8, one launch (start us, length us, event | category | flops | bytes accessed | tf_op | source)
XLA Modules:
  0.0 403.3 jit_solution(5778186779938577042)
XLA Ops:
  10.4 60.4 %while.1 = (s32[]{:T(128)}, f32[3,4224]{1,0:T(4,128)S(1)}, s32[32,2]{0,1:T(2,128)S(1)}, f32[32,3,128]{2,1,0:T(4,128)}, s32[]{:T(128)}) while((s32[]{:T(128)}, f32[3,4224]{1,0:T(4,128)S(1)}, s32[32,2]{0,1:T(2,128)S(1)}, f32[32,3,128]{2,1,0:T(4,128)}, s32[]{:T(128)}) %tuple.31), condition=%wide.while_cond, body=%wide.while_body.sunk | while | flops 2 | bytes 4197 | solution.py:53
  11.0 1.3 bitcast_dynamic-update-slice_fusion.2
  12.9 1.3 bitcast_dynamic-update-slice_fusion.2
  14.8 1.3 bitcast_dynamic-update-slice_fusion.2
  26.1 1.3 bitcast_dynamic-update-slice_fusion.2
  31.7 1.3 bitcast_dynamic-update-slice_fusion.2
  43.1 1.3 bitcast_dynamic-update-slice_fusion.2
  46.8 1.3 bitcast_dynamic-update-slice_fusion.2
  50.6 1.3 bitcast_dynamic-update-slice_fusion.2
  70.8 11.3 %all-to-all-start = ((f32[32,3,128]{2,1,0:T(4,128)}), f32[32,3,128]{2,1,0:T(4,128)S(1)}, u32[]{:S(2)}, u32[]{:S(2)}) async-start(f32[32,3,128]{2,1,0:T(4,128)} %get-tuple-element.10), calls=%async_computation | async-start | bytes 131072 | tf_op jit(solution)/shard_map/all_to_all | solution.py:56
  85.0 1.3 fusion.24
  86.4 5.7 %all-to-all-done = f32[32,3,128]{2,1,0:T(4,128)S(1)} async-done(((f32[32,3,128]{2,1,0:T(4,128)}), f32[32,3,128]{2,1,0:T(4,128)S(1)}, u32[]{:S(2)}, u32[]{:S(2)}) %all-to-all-start) | async-done | bytes 49184 | tf_op jit(solution)/shard_map/all_to_all | solution.py:56
  92.7 13.0 %gather_fusion = f32[2048,3]{1,0:T(8,128)S(1)} fusion(f32[32,3,128]{1,2,0:T(8,128)S(1)} %copy.17, s32[2048]{0:T(1024)S(1)} %bitcast.38), kind=kCustom, calls=%fused_computation | custom fusion | bytes 65536 | tf_op jit(solution)/shard_map/gather | solution.py:62
  108.2 10.1 %multiply_convert_fusion.1 = bf16[2048,1024]{1,0:T(8,128)(2,1)} fusion(f32[2048,6]{0,1:T(8,128)S(1)} %get-tuple-element.35, f32[]{:T(128)} %bitcast.10, f32[1024]{0:T(1024)S(1)} %bitcast.50, f32[2048]{0:T(1024)S(1)} %get-tuple-element.14, f32[]{:T(128)} %bitcast.8, f32[1024]{0:T(1024)S(1)} %bitcast.49, f32[2048]{0:T(1024)S(1)} %get-tuple-element.13, ...), kind=kOutput, calls=%fused_computation.6 | convolution fusion | flops 171972608 | bytes 4272136 | tf_op jit(solution)/shard_map/dot_general | solution.py:18
  118.3 7.5 %multiply_reduce_fusion = (f32[2048]{0:T(1024)S(1)}, bf16[2048,1024]{0,1:T(8,128)(2,1)S(1)}) fusion(bf16[2048,1024]{1,0:T(8,128)(2,1)} %multiply_convert_fusion.1, bf16[1024,1024]{1,0:T(8,128)(2,1)} %all-gather.3.cloned.1.call-done), kind=kOutput, calls=%fused_computation.4 | convolution fusion | flops 4301256704 | bytes 10493952 | tf_op jit(solution)/shard_map/dot_general | solution.py:78
  125.8 2.0 copy-done.1
  129.3 44.1 %all-gather.5.cloned.1.call-done = bf16[1024,1024]{1,0:T(8,128)(2,1)} async-done(((bf16[32,1024]{1,0:T(8,128)(2,1)}), bf16[1024,1024]{1,0:T(8,128)(2,1)}) %all-gather.5.cloned.1.call-update) | async-done | bytes 2097168 | tf_op jit(solution)/shard_map/all_gather | solution.py:76
  173.4 10.7 %multiply_reduce_fusion.1 = (f32[2048]{0:T(1024)S(1)}, f32[2048,1024]{0,1:T(8,128)}) fusion(bf16[2048,1024]{0,1:T(8,128)(2,1)} %copy-done.1, bf16[1024,1024]{1,0:T(8,128)(2,1)} %all-gather.5.cloned.1.call-done), kind=kOutput, calls=%fused_computation.5 | convolution fusion | flops 4299159552 | bytes 14688256 | tf_op jit(solution)/shard_map/dot_general | solution.py:80
  184.0 16.9 %psum.22 = f32[1,2048]{1,0:T(1,128)S(1)} all-reduce(f32[1,2048]{1,0:T(1,128)S(1)} %bitcast.45), channel_id=1, replica_groups=mesh['obs'=32,'ind'=8] {'ind'}, use_global_device_ids=true, to_apply=%region_8.9 | all-reduce | flops 2048 | bytes 16384 | tf_op jit(solution)/shard_map/psum | solution.py:87
  201.0 48.5 %all-reduce.4.cloned.1.call-done = f32[8,2048]{1,0:T(8,128)} async-done(((f32[8,2048]{1,0:T(8,128)}), f32[8,2048]{1,0:T(8,128)}) %all-reduce.4.cloned.1.call-update) | async-done | bytes 65552 | tf_op jit(solution)/shard_map/psum | solution.py:87
  251.4 10.7 %select_convert_fusion = bf16[1024,1024]{1,0:T(8,128)(2,1)} fusion(bf16[2048,1024]{0,1:T(8,128)(2,1)} %copy-done.1, f32[2048,1024]{0,1:T(8,128)} %get-tuple-element.37, f32[2048]{0:T(1024)S(1)} %broadcast_multiply_fusion.1), kind=kOutput, calls=%fused_computation.8 | convolution fusion | flops 4302307328 | bytes 14688256 | tf_op jit(solution)/shard_map/dot_general | solution.py:98
  262.3 3.4 fusion.12
  265.7 128.9 %psum.23 = f32[8,1024]{1,0:T(8,128)S(1)} all-reduce(f32[8,1024]{1,0:T(8,128)S(1)} %fusion.12), channel_id=1, replica_groups=mesh['obs'=32,'ind'=8] {'obs'}, use_global_device_ids=true, to_apply=%region_13.14 | all-reduce | flops 8192 | bytes 65536 | tf_op jit(solution)/shard_map/psum | solution.py:115
  395.2 1.6 fusion.7
  (142 shorter events, 63.3 us)
Async XLA Ops:
  7.2 76.2 %copy-start = (f32[6,6]{1,0:T(8,128)S(1)}, f32[6,6]{1,0:T(8,128)}, u32[]{:S(2)}) copy-start(f32[6,6]{1,0:T(8,128)} %param.16) | copy-start | bytes 436
  7.2 111.1 %all-gather.3.cloned.1.call-start = ((), (), s32[]{:S(2)}) async-start(), calls=%async_computation.2 | async-start | bytes 2162688 | tf_op jit(solution)/shard_map/all_gather | solution.py:75
  70.8 21.3 %all-to-all-start = ((f32[32,3,128]{2,1,0:T(4,128)}), f32[32,3,128]{2,1,0:T(4,128)S(1)}, u32[]{:S(2)}, u32[]{:S(2)}) async-start(f32[32,3,128]{2,1,0:T(4,128)} %get-tuple-element.10), calls=%async_computation | async-start | bytes 131072 | tf_op jit(solution)/shard_map/all_to_all | solution.py:56
  82.1 91.3 %all-gather.5.cloned.1.call-start = ((), (), s32[]{:S(2)}) async-start(), calls=%async_computation.4 | async-start | bytes 2162688 | tf_op jit(solution)/shard_map/all_gather | solution.py:76
  82.9 166.6 %all-reduce.4.cloned.1.call-start = ((), (), s32[]{:S(2)}) async-start(), calls=%async_computation.3 | async-start | bytes 131072 | tf_op jit(solution)/shard_map/psum | solution.py:87
  92.7 15.5 %copy-start.6 = (s32[1024]{0:T(1024)S(1)}, s32[1024]{0:T(1024)}, u32[]{:S(2)}) copy-start(s32[1024]{0:T(1024)} %param.15) | copy-start | bytes 12292
  118.3 9.5 %copy-start.4 = (bf16[8,1024]{1,0:T(8,128)(2,1)S(1)}, bf16[8,1024]{1,0:T(8,128)(2,1)}, u32[]{:S(2)}) copy-start(bf16[8,1024]{1,0:T(8,128)(2,1)} %param.21) | copy-start | bytes 49156
  125.8 2.0 copy-start.1
  129.1 121.3 %copy-start.5 = (f32[8]{0:T(128)S(1)}, f32[8]{0:T(128)}, u32[]{:S(2)}) copy-start(f32[8]{0:T(128)} %param.18) | copy-start | bytes 100
  129.1 266.1 %reduce-scatter.2.cloned.1.call-start = ((), (), s32[]{:S(2)}) async-start(), calls=%async_computation.5 | async-start | bytes 2162688 | tf_op jit(solution)/shard_map/reduce_scatter | solution.py:102
  251.4 10.9 %copy-start.3 = (f32[8,2048]{1,0:T(8,128)}, f32[8,2048]{1,0:T(8,128)S(1)}, u32[]{:S(2)}) copy-start(f32[8,2048]{1,0:T(8,128)S(1)} %get-tuple-element.24) | copy-start | bytes 196612
  251.4 10.7 %copy-start.2 = (bf16[32,1024]{1,0:T(8,128)(2,1)S(1)}, bf16[32,1024]{1,0:T(8,128)(2,1)}, u32[]{:S(2)}) copy-start(bf16[32,1024]{1,0:T(8,128)(2,1)} %param.20) | copy-start | bytes 196612
Sparse Core Ops, SparseCore 0:
  10.8 82.8 all-gather.2
  96.5 76.8 all-gather.4
  176.6 72.8 all-reduce.3
  262.2 120.2 reduce-scatter.1
where the time goes:
time: 405 us; the launch traced here: 403 us
  blocking collectives  146 us (36%)
  waiting for transfers between devices  99.7 us (25%)
  local copies, waits for them, and re-layouts  79.1 us (20%)
  matrix products  43.9 us (11%)
  between operations  14 us (3%)
  starting transfers between devices  11.7 us (3%)
  other arithmetic  9.17 us (2%)
    psum x1, blocking collectives, body(): lax.psum(mean_term, 'obs') - variational_mean.astype(jnp.float32)  129 us
    gather x96, local copies, waits for them, and re-layouts  60.4 us
    psum x1, waiting for transfers between devices, body(): mean_sum, var_sum = lax.psum((mean_part, var_part), 'ind')  48.5 us
    all_gather x1, waiting for transfers between devices, body(): lax.all_gather(variational_chol, 'obs', axis=0, tiled=True)  44.1 us
    psum x1, blocking collectives, body(): mean_sum, var_sum = lax.psum((mean_part, var_part), 'ind')  16.9 us
    gather x1, local copies, waits for them, and re-layouts, body(): arrived = incoming[source, :, position - begin_row].T  13 us
    all_to_all x1, starting transfers between devices, body(): lax.all_to_all(outgoing, 'obs', split_axis=0, concat_axis=0, tiled=True)  11.3 us
    dot_general x1, matrix products, body(): lax.dot_general(whitened_bf, heavy, (((0,), (0,)), ((), ())), preferred_e...  10.7 us
  transfers between devices with their start and end apart: 5, of which 3 were waited for; matrix products, arithmetic and copies ran while one was open for 29% of the time, Pallas kernels for 0%

commit v1 on v0

--- a/solution.py
+++ b/solution.py
@@ -112,7 +112,13 @@
     mean_term = lax.dot_general(
         mean_slope, whitened_bf, (((1,), (0,)), ((), ())), preferred_element_type=jnp.float32
     )
-    grad_mean = lax.psum(mean_term, "obs") - variational_mean.astype(jnp.float32)
+
+    def _work_heaps(t0, a_name):
+        kept_arr = lax.all_gather(t0, a_name)
+        small = jnp.sum(kept_arr, 0)
+        return small
+
+    grad_mean = _work_heaps(mean_term, "obs") - variational_mean.astype(jnp.float32)
     return (chances, grad_chol, grad_mean)
 
 

time: 405 us -> 464 us (1.15)
  waiting for transfers between devices: 99.7 us -> 286 us
  blocking collectives: 146 us -> 16.9 us
    psum x1 -> x0, blocking collectives: 129 us -> none  [body(): lax.psum(mean_term, 'obs') - variational_mean.astype(jnp.float32)]
    reduce_scatter x1, waiting for transfers between devices: 0.01 us -> 119 us  [body(): lax.psum_scatter(jnp.where(column_ids[None, :] <= row_ids, term, 0.0).ast...]
    all_gather x0 -> x1, waiting for transfers between devices: none -> 67.4 us  [_work_heaps(): kept_arr = lax.all_gather(t0, a_name)]
  transfers between devices with their start and end apart: 5 -> 6, of which waited for: 3 -> 5; matrix products, arithmetic and copies ran while one was open for 29% -> 27% of each run, Pallas kernels for 0% -> 0%
where the time goes in v1:
time: 464 us; the launch traced here: 463 us
  waiting for transfers between devices  286 us (62%)
  local copies, waits for them, and re-layouts  79.1 us (17%)
  matrix products  44.6 us (10%)
  blocking collectives  16.9 us (4%)
  between operations  14 us (3%)
  starting transfers between devices  11.7 us (3%)
  other arithmetic  10.5 us (2%)
    reduce_scatter x1, waiting for transfers between devices, body(): lax.psum_scatter(jnp.where(column_ids[None, :] <= row_ids, term, 0.0).ast...  119 us
    all_gather x1, waiting for transfers between devices, _work_heaps(): kept_arr = lax.all_gather(t0, a_name)  67.4 us
    gather x96, local copies, waits for them, and re-layouts  60.4 us
    psum x1, waiting for transfers between devices, body(): mean_sum, var_sum = lax.psum((mean_part, var_part), 'ind')  48.5 us
    all_gather x1, waiting for transfers between devices, body(): lax.all_gather(variational_chol, 'obs', axis=0, tiled=True)  44 us
    psum x1, blocking collectives, body(): mean_sum, var_sum = lax.psum((mean_part, var_part), 'ind')  16.9 us
    gather x1, local copies, waits for them, and re-layouts, body(): arrived = incoming[source, :, position - begin_row].T  13 us
    all_to_all x1, starting transfers between devices, body(): lax.all_to_all(outgoing, 'obs', split_axis=0, concat_axis=0, tiled=True)  11.3 us
  transfers between devices with their start and end apart: 6, of which 5 were waited for; matrix products, arithmetic and copies ran while one was open for 27% of the time, Pallas kernels for 0%

profile of v1, /device:TPU:8, one launch (start us, length us, event | category | flops | bytes accessed | tf_op | source)
XLA Modules:
  0.0 462.6 jit_solution(15563889690973314078)
XLA Ops:
  10.4 60.4 %while.1 = (s32[]{:T(128)}, f32[3,4224]{1,0:T(4,128)S(1)}, s32[32,2]{0,1:T(2,128)S(1)}, f32[32,3,128]{2,1,0:T(4,128)}, s32[]{:T(128)}) while((s32[]{:T(128)}, f32[3,4224]{1,0:T(4,128)S(1)}, s32[32,2]{0,1:T(2,128)S(1)}, f32[32,3,128]{2,1,0:T(4,128)}, s32[]{:T(128)}) %tuple.31), condition=%wide.while_cond, body=%wide.while_body.sunk | while | flops 2 | bytes 4197 | solution.py:53
  11.0 1.3 bitcast_dynamic-update-slice_fusion.2
  12.9 1.3 bitcast_dynamic-update-slice_fusion.2
  14.8 1.3 bitcast_dynamic-update-slice_fusion.2
  31.7 1.3 bitcast_dynamic-update-slice_fusion.2
  43.1 1.3 bitcast_dynamic-update-slice_fusion.2
  46.8 1.3 bitcast_dynamic-update-slice_fusion.2
  50.6 1.3 bitcast_dynamic-update-slice_fusion.2
  70.8 11.3 %all-to-all-start = ((f32[32,3,128]{2,1,0:T(4,128)}), f32[32,3,128]{2,1,0:T(4,128)S(1)}, u32[]{:S(2)}, u32[]{:S(2)}) async-start(f32[32,3,128]{2,1,0:T(4,128)} %get-tuple-element.10), calls=%async_computation | async-start | bytes 131072 | tf_op jit(solution)/shard_map/all_to_all | solution.py:56
  85.0 1.3 fusion.24
  86.4 5.7 %all-to-all-done = f32[32,3,128]{2,1,0:T(4,128)S(1)} async-done(((f32[32,3,128]{2,1,0:T(4,128)}), f32[32,3,128]{2,1,0:T(4,128)S(1)}, u32[]{:S(2)}, u32[]{:S(2)}) %all-to-all-start) | async-done | bytes 49184 | tf_op jit(solution)/shard_map/all_to_all | solution.py:56
  92.7 13.0 %gather_fusion = f32[2048,3]{1,0:T(8,128)S(1)} fusion(f32[32,3,128]{1,2,0:T(8,128)S(1)} %copy.17, s32[2048]{0:T(1024)S(1)} %bitcast.40), kind=kCustom, calls=%fused_computation | custom fusion | bytes 65536 | tf_op jit(solution)/shard_map/gather | solution.py:62
  108.2 10.1 %multiply_convert_fusion.1 = bf16[2048,1024]{1,0:T(8,128)(2,1)} fusion(f32[2048,6]{0,1:T(8,128)S(1)} %get-tuple-element.35, f32[]{:T(128)} %bitcast.10, f32[1024]{0:T(1024)S(1)} %bitcast.52, f32[2048]{0:T(1024)S(1)} %get-tuple-element.14, f32[]{:T(128)} %bitcast.8, f32[1024]{0:T(1024)S(1)} %bitcast.51, f32[2048]{0:T(1024)S(1)} %get-tuple-element.13, ...), kind=kOutput, calls=%fused_computation.6 | convolution fusion | flops 171972608 | bytes 4272136 | tf_op jit(solution)/shard_map/dot_general | solution.py:18
  118.3 7.5 %multiply_reduce_fusion = (f32[2048]{0:T(1024)S(1)}, bf16[2048,1024]{0,1:T(8,128)(2,1)S(1)}) fusion(bf16[2048,1024]{1,0:T(8,128)(2,1)} %multiply_convert_fusion.1, bf16[1024,1024]{1,0:T(8,128)(2,1)} %all-gather.5.cloned.1.call-done), kind=kOutput, calls=%fused_computation.4 | convolution fusion | flops 4301256704 | bytes 10493952 | tf_op jit(solution)/shard_map/dot_general | solution.py:78
  125.8 2.0 copy-done.1
  129.3 44.0 %all-gather.7.cloned.1.call-done = bf16[1024,1024]{1,0:T(8,128)(2,1)} async-done(((bf16[32,1024]{1,0:T(8,128)(2,1)}), bf16[1024,1024]{1,0:T(8,128)(2,1)}) %all-gather.7.cloned.1.call-update) | async-done | bytes 2097168 | tf_op jit(solution)/shard_map/all_gather | solution.py:76
  173.4 10.7 %multiply_reduce_fusion.1 = (f32[2048]{0:T(1024)S(1)}, f32[2048,1024]{0,1:T(8,128)}) fusion(bf16[2048,1024]{0,1:T(8,128)(2,1)} %copy-done.1, bf16[1024,1024]{1,0:T(8,128)(2,1)} %all-gather.7.cloned.1.call-done), kind=kOutput, calls=%fused_computation.5 | convolution fusion | flops 4299159552 | bytes 14688256 | tf_op jit(solution)/shard_map/dot_general | solution.py:80
  184.0 16.9 %psum.15 = f32[1,2048]{1,0:T(1,128)S(1)} all-reduce(f32[1,2048]{1,0:T(1,128)S(1)} %bitcast.47), channel_id=1, replica_groups=mesh['obs'=32,'ind'=8] {'ind'}, use_global_device_ids=true, to_apply=%region_8.9 | all-reduce | flops 2048 | bytes 16384 | tf_op jit(solution)/shard_map/psum | solution.py:87
  201.0 48.5 %all-reduce.4.cloned.1.call-done = f32[8,2048]{1,0:T(8,128)} async-done(((f32[8,2048]{1,0:T(8,128)}), f32[8,2048]{1,0:T(8,128)}) %all-reduce.4.cloned.1.call-update) | async-done | bytes 65552 | tf_op jit(solution)/shard_map/psum | solution.py:87
  251.4 4.0 fusion.12
  255.5 10.7 %select_convert_fusion = bf16[1024,1024]{1,0:T(8,128)(2,1)} fusion(bf16[2048,1024]{0,1:T(8,128)(2,1)} %copy-done.1, f32[2048,1024]{0,1:T(8,128)} %get-tuple-element.37, f32[2048]{0:T(1024)S(1)} %broadcast_multiply_fusion.1), kind=kOutput, calls=%fused_computation.8 | convolution fusion | flops 4302307328 | bytes 14688256 | tf_op jit(solution)/shard_map/dot_general | solution.py:98
  266.4 67.4 %all-gather.9.cloned.1.call-done = f32[256,1024]{1,0:T(8,128)} async-done(((f32[8,1024]{1,0:T(8,128)}), f32[256,1024]{1,0:T(8,128)}) %all-gather.9.cloned.1.call-update) | async-done | bytes 1048592 | tf_op jit(solution)/shard_map/all_gather | solution.py:117
  335.7 118.9 %reduce-scatter.2.cloned.1.call-done = bf16[32,1024]{1,0:T(8,128)(2,1)} async-done(((bf16[1024,1024]{1,0:T(8,128)(2,1)}), bf16[32,1024]{1,0:T(8,128)(2,1)}) %reduce-scatter.2.cloned.1.call-update) | async-done | bytes 65552 | tf_op jit(solution)/shard_map/reduce_scatter | solution.py:102
  454.5 1.6 fusion.7
  (145 shorter events, 66.0 us)
Async XLA Ops:
  7.2 76.2 %copy-start = (f32[6,6]{1,0:T(8,128)S(1)}, f32[6,6]{1,0:T(8,128)}, u32[]{:S(2)}) copy-start(f32[6,6]{1,0:T(8,128)} %param.16) | copy-start | bytes 436
  7.2 111.1 %all-gather.5.cloned.1.call-start = ((), (), s32[]{:S(2)}) async-start(), calls=%async_computation.2 | async-start | bytes 2162688 | tf_op jit(solution)/shard_map/all_gather | solution.py:75
  70.8 21.3 %all-to-all-start = ((f32[32,3,128]{2,1,0:T(4,128)}), f32[32,3,128]{2,1,0:T(4,128)S(1)}, u32[]{:S(2)}, u32[]{:S(2)}) async-start(f32[32,3,128]{2,1,0:T(4,128)} %get-tuple-element.10), calls=%async_computation | async-start | bytes 131072 | tf_op jit(solution)/shard_map/all_to_all | solution.py:56
  82.1 91.3 %all-gather.7.cloned.1.call-start = ((), (), s32[]{:S(2)}) async-start(), calls=%async_computation.4 | async-start | bytes 2162688 | tf_op jit(solution)/shard_map/all_gather | solution.py:76
  82.9 166.6 %all-reduce.4.cloned.1.call-start = ((), (), s32[]{:S(2)}) async-start(), calls=%async_computation.3 | async-start | bytes 131072 | tf_op jit(solution)/shard_map/psum | solution.py:87
  92.7 15.5 %copy-start.6 = (s32[1024]{0:T(1024)S(1)}, s32[1024]{0:T(1024)}, u32[]{:S(2)}) copy-start(s32[1024]{0:T(1024)} %param.15) | copy-start | bytes 12292
  118.3 9.5 %copy-start.4 = (bf16[8,1024]{1,0:T(8,128)(2,1)S(1)}, bf16[8,1024]{1,0:T(8,128)(2,1)}, u32[]{:S(2)}) copy-start(bf16[8,1024]{1,0:T(8,128)(2,1)} %param.21) | copy-start | bytes 49156
  125.8 2.0 copy-start.1
  129.1 121.3 %copy-start.5 = (f32[8]{0:T(128)S(1)}, f32[8]{0:T(128)}, u32[]{:S(2)}) copy-start(f32[8]{0:T(128)} %param.18) | copy-start | bytes 100
  129.1 204.7 %all-gather.9.cloned.1.call-start = ((), (), s32[]{:S(2)}) async-start(), calls=%async_computation.6 | async-start | bytes 1081344 | tf_op jit(solution)/shard_map/all_gather | solution.py:117
  251.4 14.8 %copy-start.3 = (f32[8,2048]{1,0:T(8,128)}, f32[8,2048]{1,0:T(8,128)S(1)}, u32[]{:S(2)}) copy-start(f32[8,2048]{1,0:T(8,128)S(1)} %get-tuple-element.24) | copy-start | bytes 196612
  255.4 199.1 %reduce-scatter.2.cloned.1.call-start = ((), (), s32[]{:S(2)}) async-start(), calls=%async_computation.5 | async-start | bytes 2162688 | tf_op jit(solution)/shard_map/reduce_scatter | solution.py:102
  255.5 10.7 %copy-start.2 = (bf16[32,1024]{1,0:T(8,128)(2,1)S(1)}, bf16[32,1024]{1,0:T(8,128)(2,1)}, u32[]{:S(2)}) copy-start(bf16[32,1024]{1,0:T(8,128)(2,1)} %param.20) | copy-start | bytes 196612
Sparse Core Ops, SparseCore 0:
  10.8 82.8 all-gather.4
  96.5 76.8 all-gather.6
  176.6 72.8 all-reduce.3
  255.5 78.1 all-gather.8
  338.3 116.1 reduce-scatter.1
